TPU v7x, 128 devices: a whole 4x4x4 slice. The times are simulated.
128 devices in a mesh: tm: 4 (over x), op: 32 (over y, z, core).
Axes of the slice: x: 4, y: 4, z: 4, core: 2. Of those that a mesh axis runs over, the one named last changes fastest.
Arguments:
- sink_elem: bfloat16 [2, 4, 2048, 16384], P(None, 'tm', 'op'), may hold values from -6 to 6
- source_elem: bfloat16 [2, 2, 2048, 16384], P(None, None, None, 'op'), may hold values from -6 to 6
- peram: bfloat16 [2, 4, 2, 512, 512], P(None, 'tm', None, 'op'), may hold values from -4 to 4
- pair_list: int32 [16, 1], replicated, may hold values from 0 to 15
- spin_sets: int32 [16, 3], replicated, may hold values from 0 to 3
Outputs:
- correlator: float32 [2, 4, 2, 16, 1], P(None, 'tm')
All inputs are finite; a program needn't handle non-finite values.
Results may differ from a plain program's by a relative error of at most 0.0041.
Values may be sent and summed in bfloat16 or wider, within the bound.
A program may use at most 192 MiB of HBM per device.

v0:
```python
import jax
import jax.numpy as jnp
from jax import lax
from jax.sharding import PartitionSpec as P

NEV = 128
NSPIN = 4
NOP = 16
TSRC = 2
PAIRS = 1


def complex_matrix(block):
    upper = jnp.concatenate([block[0], block[1]], axis=1)
    lower = jnp.concatenate([-block[1], block[0]], axis=1)
    return jnp.stack([upper, lower])


def on_device(sink_elem, source_elem, peram, pair_list, spin_sets):
    tau_all = lax.all_gather(peram, "op", axis=3, tiled=True)
    position = lax.axis_index("op")
    rows = sink_elem.shape[2]
    local_times = sink_elem.shape[1]
    span = min(rows, NEV)
    cols = source_elem.shape[3]

    def spin_block(local, t0, left, right):
        return lax.dynamic_slice(tau_all[:, local, t0], (0, left * NEV, right * NEV), (2, NEV, NEV))

    def sink_side(local, t0, p):
        op_now = (position * rows + 0) // NEV
        mine = spin_sets[op_now]
        theirs = spin_sets[pair_list[op_now, p]]
        third = complex_matrix(spin_block(local, t0, mine[2], theirs[2]))
        second = complex_matrix(spin_block(local, t0, mine[1], theirs[1]))
        phi = sink_elem[:, local, 0:span].reshape(2, span * NEV, NEV)
        x_both = jnp.einsum("cxk,ckb->xb", phi, third, preferred_element_type=jnp.float32)
        x_both = x_both.astype(jnp.bfloat16).reshape(span, NEV, 2, NEV)
        y_both = jnp.einsum("ijck,cjb->ibk", x_both, second, preferred_element_type=jnp.float32)
        y_both = y_both.astype(jnp.bfloat16).reshape(span, 2, NEV * NEV)
        pieces = jnp.transpose(y_both, (1, 0, 2))
        return pieces

    partial_terms = {}
    combos = [
        (local, t0, p) for local in range(local_times) for t0 in range(TSRC) for p in range(PAIRS)
    ]
    stacked = jnp.stack([sink_side(local, t0, p) for local, t0, p in combos], axis=1)
    columns = lax.all_to_all(stacked, "op", split_axis=3, concat_axis=2, tiled=True)
    for index, combo in enumerate(combos):
        column_t0 = combo[1]
        other = pair_list[:, combo[2]]
        source = source_elem[:, column_t0].reshape(2, NOP, NEV, cols)
        chosen = jnp.take(source, other, axis=1)
        tiles = columns[:, index].reshape(2, NOP, NEV, cols)

        def inner(a, b):
            return jnp.einsum("oic,ojc->oij", a, b, preferred_element_type=jnp.float32)

        m_re = inner(tiles[0], chosen[0]) + inner(tiles[1], chosen[1])
        m_im = inner(tiles[1], chosen[0]) - inner(tiles[0], chosen[1])
        blocks = tau_all[:, combo[0], column_t0].reshape(2, NSPIN, NEV, NSPIN, NEV)
        blocks = jnp.transpose(blocks, (1, 3, 0, 2, 4))
        first = blocks[spin_sets[:, 0], spin_sets[other, 0]].astype(jnp.float32)
        c_re = jnp.sum(first[:, 0] * m_re - first[:, 1] * m_im, axis=(1, 2))
        c_im = jnp.sum(first[:, 0] * m_im + first[:, 1] * m_re, axis=(1, 2))
        partial_terms[combo] = jnp.stack([c_re, c_im])
    local = 0
    per_time = []
    for t0 in range(TSRC):
        per_time.append(jnp.stack([partial_terms[local, t0, 0]], axis=-1))
    per_local = [jnp.stack(per_time, axis=1)]
    partial_sum = jnp.stack(per_local, axis=1)
    totals = lax.psum(partial_sum, "op")
    return totals * (1.0 / float(NEV**3))


def solution(mesh):
    in_specs = (
        P(None, "tm", "op", None),
        P(None, None, None, "op"),
        P(None, "tm", None, "op", None),
        P(),
        P(),
    )
    out_specs = P(None, "tm", None, None, None)
    return jax.shard_map(
        on_device, mesh=mesh, in_specs=in_specs, out_specs=out_specs, check_vma=False
    )
```

profile of v0, /device:TPU:1, one launch (start us, length us, event | category | flops | bytes accessed | tf_op | source)
XLA Modules:
  0.0 462.1 jit_solution(5356037397111504323)
XLA Ops:
  6.5 1.5 copy.40
  15.2 7.4 %reshape_squeeze.19 = bf16[2,8192,128]{2,1,0:T(8,128)(2,1)} reshape(bf16[2,1,64,16384]{3,2,1,0:T(8,128)(2,1)} %param.7) | data formatting | bytes 8388608 | tf_op jit(solution)/shard_map/reshape;squeeze | solution.py:36
  22.6 34.7 %all-gather.2.cloned.1.call-done = bf16[2,1,2,512,512]{4,2,1,0,3:T(2,128)(2,1)} async-done(((bf16[2,1,2,16,512]{4,2,1,0,3:T(2,128)(2,1)}), bf16[2,1,2,512,512]{4,2,1,0,3:T(2,128)(2,1)}) %all-gather.2.cloned.1.call-update) | async-done | bytes 2097168 | tf_op jit(solution)/shard_map/all_gather | solution.py:20
  57.3 6.5 %fusion.57 = (bf16[2,1,1,512,512]{4,2,1,0,3:T(2,128)(2,1)}, bf16[2,1,1,512,512]{4,2,1,0,3:T(2,128)(2,1)S(1)}) fusion(bf16[2,1,2,512,512]{4,2,1,0,3:T(2,128)(2,1)} %all-gather.2.cloned.1.call-done), kind=kLoop, calls=%fused_computation.113 | loop fusion | bytes 4194304 | tf_op jit(solution)/shard_map/slice | solution.py:62
  63.8 4.6 copy.59
  68.4 4.2 copy.60
  74.2 3.5 fusion.15
  78.9 7.4 %fusion.2 = bf16[64,256,128]{2,1,0:T(8,128)(2,1)} fusion(bf16[64,128,2,128]{1,0,3,2:T(8,128)(2,1)S(1)} %bitcast.218, bf16[1,128,256]{1,2,0:T(8,128)(2,1)S(1)} %get-tuple-element.35, bf16[1,128,256]{1,2,0:T(8,128)(2,1)S(1)} %get-tuple-element.34), kind=kOutput, calls=%fused_computation.12 | convolution fusion | flops 1076101120 | bytes 8519680 | tf_op jit(solution)/shard_map/ijck,cjb->ibk/dot_general | solution.py:39
  86.4 6.9 %reshape.75 = bf16[64,2,16384]{2,1,0:T(2,128)(2,1)} reshape(bf16[64,256,128]{2,1,0:T(8,128)(2,1)} %fusion.2) | data formatting | bytes 8388608 | tf_op jit(solution)/shard_map/reshape | solution.py:40
  93.2 6.6 %copy.83 = bf16[64,2,16384]{2,0,1:T(8,128)(2,1)} copy(bf16[64,2,16384]{2,1,0:T(2,128)(2,1)} %reshape.75) | data formatting | bytes 8388608 | tf_op jit(solution)/shard_map/reshape | solution.py:40
  102.4 7.4 %fusion.3 = bf16[64,256,128]{2,1,0:T(8,128)(2,1)} fusion(bf16[64,128,2,128]{1,0,3,2:T(8,128)(2,1)S(1)} %bitcast.219, bf16[1,128,256]{1,2,0:T(8,128)(2,1)S(1)} %get-tuple-element.39, bf16[1,128,256]{1,2,0:T(8,128)(2,1)S(1)} %get-tuple-element.38), kind=kOutput, calls=%fused_computation.13 | convolution fusion | flops 1076101120 | bytes 8519680 | tf_op jit(solution)/shard_map/ijck,cjb->ibk/dot_general | solution.py:39
  109.8 6.9 %reshape.77 = bf16[64,2,16384]{2,1,0:T(2,128)(2,1)} reshape(bf16[64,256,128]{2,1,0:T(8,128)(2,1)} %fusion.3) | data formatting | bytes 8388608 | tf_op jit(solution)/shard_map/reshape | solution.py:40
  116.7 6.6 %copy.82 = bf16[64,2,16384]{2,0,1:T(8,128)(2,1)} copy(bf16[64,2,16384]{2,1,0:T(2,128)(2,1)} %reshape.77) | data formatting | bytes 8388608 | tf_op jit(solution)/shard_map/reshape | solution.py:40
  123.3 6.2 %pad_maximum_fusion = bf16[2,2,64,16384]{3,2,1,0:T(8,128)(2,1)} fusion(bf16[2,1,64,16384]{3,2,1,0:T(8,128)(2,1)} %bitcast.222, bf16[2,1,64,16384]{3,2,1,0:T(8,128)(2,1)S(1)} %bitcast.220), kind=kLoop, calls=%fused_computation.9 | loop fusion | flops 4194304 | bytes 16777216 | tf_op jit(solution)/shard_map/stack | solution.py:48
  129.5 34.5 %copy.49 = bf16[2,2,64,16384]{2,1,0,3:T(2,128)(2,1)} copy(bf16[2,2,64,16384]{3,2,1,0:T(8,128)(2,1)} %pad_maximum_fusion) | data formatting | bytes 16777216 | tf_op jit(solution)/shard_map/stack | solution.py:48
  164.0 26.7 %reshape.124 = bf16[32,2,65536]{2,1,0:T(2,128)(2,1)} reshape(bf16[16384,2,2,64]{3,2,1,0:T(2,128)(2,1)} %bitcast.211) | data formatting | bytes 16777216
  190.7 5.4 %all-to-all-start = ((bf16[32,2,65536]{2,1,0:T(2,128)(2,1)}), bf16[32,2,65536]{2,1,0:T(2,128)(2,1)}, u32[]{:S(2)}, u32[]{:S(2)}) async-start(bf16[32,2,65536]{2,1,0:T(2,128)(2,1)} %reshape.124), calls=%async_computation | async-start | bytes 16777216 | tf_op jit(solution)/shard_map/all_to_all | solution.py:49
  196.2 5.8 %fusion.56 = (bf16[2,1,2048,512]{3,2,1,0:T(8,128)(2,1)}, bf16[2,1,2048,512]{3,2,1,0:T(8,128)(2,1)}) fusion(bf16[2,2,2048,512]{3,2,1,0:T(8,128)(2,1)} %param.8), kind=kLoop, calls=%fused_computation.112 | loop fusion | bytes 16777216 | tf_op jit(solution)/shard_map/slice | solution.py:53
  202.0 5.0 %gather_fusion.3 = bf16[16,2,128,512]{3,2,1,0:T(8,128)(2,1)} fusion(bf16[2,16,128,512]{3,2,1,0:T(8,128)(2,1)} %bitcast.223, s32[1024]{0:T(1024)S(1)} %pad_clamp_fusion), kind=kCustom, calls=%fused_computation.clone | custom fusion | bytes 8388672 | tf_op jit(solution)/shard_map/jit(_take)/gather | solution.py:54
  207.0 5.0 %gather_fusion.4 = bf16[16,2,128,512]{3,2,1,0:T(8,128)(2,1)} fusion(bf16[2,16,128,512]{3,2,1,0:T(8,128)(2,1)} %bitcast.221, s32[1024]{0:T(1024)S(1)} %pad_clamp_fusion), kind=kCustom, calls=%fused_computation.1.clone | custom fusion | bytes 8388672 | tf_op jit(solution)/shard_map/jit(_take)/gather | solution.py:54
  212.7 6.0 %fusion.5 = (bf16[2,16,128,512]{3,2,1,0:T(8,128)(2,1)}, bf16[2,16,128,512]{3,2,1,0:T(8,128)(2,1)}) fusion(bf16[16,2,128,512]{3,2,1,0:T(8,128)(2,1)} %gather_fusion.3, pred[16]{0:T(512)(128)(4,1)S(1)} %compare_and_fusion, bf16[16,2,128,512]{3,2,1,0:T(8,128)(2,1)} %gather_fusion.4), kind=kLoop, calls=%fused_computation.17 | loop fusion | flops 4194304 | bytes 16777232 | tf_op jit(solution)/shard_map/jit(_take)/select_n | solution.py:54
  220.1 1.5 copy.42
  221.6 1.7 copy.52
  223.3 2.0 gather_fusion.1
  226.0 1.5 copy_convert_fusion.1
  227.6 1.6 copy_convert_fusion
  229.2 75.5 %all-to-all-done = bf16[32,2,65536]{2,1,0:T(2,128)(2,1)} async-done(((bf16[32,2,65536]{2,1,0:T(2,128)(2,1)}), bf16[32,2,65536]{2,1,0:T(2,128)(2,1)}, u32[]{:S(2)}, u32[]{:S(2)}) %all-to-all-start) | async-done | bytes 8388640 | tf_op jit(solution)/shard_map/all_to_all | solution.py:49
  304.7 26.0 %reshape.125 = bf16[16384,2,2,64]{3,2,1,0:T(2,128)(2,1)} reshape(bf16[32,2,65536]{2,1,0:T(2,128)(2,1)} %all-to-all-done) | data formatting | bytes 16777216
  330.7 36.1 %copy.50 = bf16[2,2,32,64,512]{4,3,2,1,0:T(8,128)(2,1)} copy(bf16[2,2,32,64,512]{3,1,0,4,2:T(2,128)(2,1)} %bitcast.212) | data formatting | bytes 16777216 | tf_op jit(solution)/shard_map/all_to_all | solution.py:49
  366.8 4.0 fusion.55
  373.6 1.4 copy-done.2
  380.5 74.2 %psum.7 = f32[2,1,2,16,1]{3,2,0,4,1:T(2,128)S(1)} all-reduce(f32[2,1,2,16,1]{3,2,0,4,1:T(2,128)S(1)} %bitcast.230), channel_id=1, replica_groups=mesh['tm'=4,'op'=32] {'op'}, use_global_device_ids=true, to_apply=%region_4.6 | all-reduce | flops 64 | bytes 512 | tf_op jit(solution)/shard_map/psum | solution.py:74
  (55 shorter events, 19.8 us)
Async XLA Ops:
  6.5 50.8 %all-gather.2.cloned.1.call-start = ((), (), s32[]{:S(2)}) async-start(), calls=%async_computation.1 | async-start | bytes 2162688 | tf_op jit(solution)/shard_map/all_gather | solution.py:20
  93.2 6.6 %copy-start.1 = (bf16[2,8192,128]{2,1,0:T(8,128)(2,1)S(1)}, bf16[2,8192,128]{2,1,0:T(8,128)(2,1)}, u32[]{:S(2)}) copy-start(bf16[2,8192,128]{2,1,0:T(8,128)(2,1)} %reshape_squeeze.19) | copy-start | bytes 12582916
  116.7 6.6 %copy-start.4 = (bf16[64,2,16384]{2,0,1:T(8,128)(2,1)S(1)}, bf16[64,2,16384]{2,0,1:T(8,128)(2,1)}, u32[]{:S(2)}) copy-start(bf16[64,2,16384]{2,0,1:T(8,128)(2,1)} %copy.83) | copy-start | bytes 12582916
  190.7 5.4 %copy-start.8 = (s32[16,1]{0,1:T(1,128)S(1)}, s32[16,1]{0,1:T(1,128)}, u32[]{:S(2)}) copy-start(s32[16,1]{0,1:T(1,128)} %param.10) | copy-start | bytes 196
  190.7 114.0 %all-to-all-start = ((bf16[32,2,65536]{2,1,0:T(2,128)(2,1)}), bf16[32,2,65536]{2,1,0:T(2,128)(2,1)}, u32[]{:S(2)}, u32[]{:S(2)}) async-start(bf16[32,2,65536]{2,1,0:T(2,128)(2,1)} %reshape.124), calls=%async_computation | async-start | bytes 16777216 | tf_op jit(solution)/shard_map/all_to_all | solution.py:49
  207.0 5.0 %copy-start = (s32[16,3]{0,1:T(4,128)S(1)}, s32[16,3]{0,1:T(4,128)}, u32[]{:S(2)}) copy-start(s32[16,3]{0,1:T(4,128)} %param.11) | copy-start | bytes 580
  212.7 6.3 %copy-start.5 = (bf16[2,1,1,512,512]{3,4,2,1,0:T(8,128)(2,1)S(1)}, bf16[2,1,1,512,512]{3,4,2,1,0:T(8,128)(2,1)}, u32[]{:S(2)}) copy-start(bf16[2,1,1,512,512]{3,4,2,1,0:T(8,128)(2,1)} %copy.60) | copy-start | bytes 3145732
  366.8 4.7 %copy-start.3 = (bf16[2,16,128,512]{3,2,1,0:T(8,128)(2,1)S(1)}, bf16[2,16,128,512]{3,2,1,0:T(8,128)(2,1)}, u32[]{:S(2)}) copy-start(bf16[2,16,128,512]{3,2,1,0:T(8,128)(2,1)} %get-tuple-element.48) | copy-start | bytes 12582916
  372.8 2.2 copy-start.2
  376.5 1.6 copy-start.7
  378.0 1.6 copy-start.6
Sparse Core Ops, SparseCore 0:
  9.6 47.6 all-gather.1
where the time goes:
time: 467 us; the launch traced here: 462 us
  local copies, waits for them, and re-layouts  212 us (45%)
  waiting for transfers between devices  110 us (24%)
  blocking collectives  74.2 us (16%)
  matrix products  25.6 us (5%)
  between operations  18.1 us (4%)
  other arithmetic  16.8 us (4%)
  starting transfers between devices  5.43 us (1%)
    all_to_all x1, waiting for transfers between devices, on_device(): lax.all_to_all(stacked, 'op', split_axis=3, concat_axis=2, tiled=True)  75.5 us
    psum x1, blocking collectives, on_device(): totals = lax.psum(partial_sum, 'op')  74.2 us
    unnamed x25, local copies, waits for them, and re-layouts  69.1 us
    all_to_all x1, local copies, waits for them, and re-layouts, on_device(): lax.all_to_all(stacked, 'op', split_axis=3, concat_axis=2, tiled=True)  36.1 us
    all_gather x1, waiting for transfers between devices, on_device(): tau_all = lax.all_gather(peram, 'op', axis=3, tiled=True)  34.7 us
    another operation x1, local copies, waits for them, and re-layouts, on_device(): jnp.stack([sink_side(local, t0, p) for local, t0, p in combos], axis=1)  34.5 us
    reshape x4, local copies, waits for them, and re-layouts, sink_side(): y_both = y_both.astype(jnp.bfloat16).reshape(span, 2, NEV * NEV)  27 us
    dot_general x2, matrix products, sink_side(): jnp.einsum('ijck,cjb->ibk', x_both, second, preferred_element_type=jnp.fl...  14.9 us
  transfers between devices with their start and end apart: 2, of which 2 were waited for; matrix products, arithmetic and copies ran while one was open for 9% of the time, Pallas kernels for 0%

commit v1 on v0

--- a/solution.py
+++ b/solution.py
@@ -17,7 +17,13 @@
 
 
 def on_device(sink_elem, source_elem, peram, pair_list, spin_sets):
-    tau_all = lax.all_gather(peram, "op", axis=3, tiled=True)
+
+    def indices_feed(matrix):
+        d_next = jnp.stack([matrix for _ in range(lax.axis_size("op"))], axis=0)
+        arr_out = lax.all_to_all(d_next, "op", 0, 0)
+        return jnp.concatenate(arr_out, axis=3)
+
+    tau_all = indices_feed(peram)
     position = lax.axis_index("op")
     rows = sink_elem.shape[2]
     local_times = sink_elem.shape[1]

time: 467 us -> 429 us (0.919)
  waiting for transfers between devices: 110 us -> 91 us
  local copies, waits for them, and re-layouts: 212 us -> 197 us
  between operations: 18.1 us -> 4.76 us
  starting transfers between devices: 5.43 us -> 15 us
    all_gather x1 -> x0, waiting for transfers between devices: 34.7 us -> none  [on_device(): tau_all = lax.all_gather(peram, 'op', axis=3, tiled=True)]
    all_to_all x0 -> x1, waiting for transfers between devices: none -> 15.2 us  [indices_feed(): arr_out = lax.all_to_all(d_next, 'op', 0, 0)]
    all_to_all x0 -> x1, starting transfers between devices: none -> 9.6 us  [indices_feed(): arr_out = lax.all_to_all(d_next, 'op', 0, 0)]
    unnamed x25 -> x22, local copies, waits for them, and re-layouts: 69.1 us -> 60.9 us
    slice x1, local copies, waits for them, and re-layouts: 6.48 us -> 1.16 us  [on_device(): blocks = tau_all[:, combo[0], column_t0].reshape(2, NSPIN, NEV, NSPIN, NEV)]
where the time goes in v1:
time: 429 us; the launch traced here: 425 us
  local copies, waits for them, and re-layouts  197 us (46%)
  waiting for transfers between devices  91 us (21%)
  blocking collectives  75.7 us (18%)
  matrix products  25.6 us (6%)
  other arithmetic  16 us (4%)
  starting transfers between devices  15 us (3%)
  between operations  4.76 us (1%)
    all_to_all x1, waiting for transfers between devices, on_device(): lax.all_to_all(stacked, 'op', split_axis=3, concat_axis=2, tiled=True)  75.8 us
    psum x1, blocking collectives, on_device(): totals = lax.psum(partial_sum, 'op')  75.7 us
    unnamed x22, local copies, waits for them, and re-layouts  60.9 us
    all_to_all x1, local copies, waits for them, and re-layouts, on_device(): lax.all_to_all(stacked, 'op', split_axis=3, concat_axis=2, tiled=True)  36 us
    another operation x1, local copies, waits for them, and re-layouts, on_device(): jnp.stack([sink_side(local, t0, p) for local, t0, p in combos], axis=1)  34.5 us
    reshape x4, local copies, waits for them, and re-layouts, sink_side(): y_both = y_both.astype(jnp.bfloat16).reshape(span, 2, NEV * NEV)  27 us
    all_to_all x1, waiting for transfers between devices, indices_feed(): arr_out = lax.all_to_all(d_next, 'op', 0, 0)  15.2 us
    dot_general x2, matrix products, sink_side(): jnp.einsum('ijck,cjb->ibk', x_both, second, preferred_element_type=jnp.fl...  14.9 us
  transfers between devices with their start and end apart: 2, of which 2 were waited for; matrix products, arithmetic and copies ran while one was open for 9% of the time, Pallas kernels for 0%

profile of v1, /device:TPU:1, one launch (start us, length us, event | category | flops | bytes accessed | tf_op | source)
XLA Modules:
  0.0 424.7 jit_solution(8503525131336484363)
XLA Ops:
  0.0 2.5 stack.48
  2.5 9.6 %all-to-all-start = ((bf16[32,2,1,2,16,512]{5,4,3,1,2,0:T(8,128)(2,1)}), bf16[32,2,1,2,16,512]{5,4,3,1,2,0:T(8,128)(2,1)S(1)}, u32[]{:S(2)}, u32[]{:S(2)}) async-start(bf16[32,2,1,2,16,512]{5,4,3,1,2,0:T(8,128)(2,1)} %stack.48), calls=%async_computation | async-start | bytes 4194304 | tf_op jit(solution)/shard_map/all_to_all | solution.py:23
  17.8 7.4 %reshape_squeeze.19 = bf16[2,8192,128]{2,1,0:T(8,128)(2,1)} reshape(bf16[2,1,64,16384]{3,2,1,0:T(8,128)(2,1)} %param.7) | data formatting | bytes 8388608 | tf_op jit(solution)/shard_map/reshape;squeeze | solution.py:42
  25.2 15.2 %all-to-all-done = bf16[32,2,1,2,16,512]{5,4,3,1,2,0:T(8,128)(2,1)S(1)} async-done(((bf16[32,2,1,2,16,512]{5,4,3,1,2,0:T(8,128)(2,1)}), bf16[32,2,1,2,16,512]{5,4,3,1,2,0:T(8,128)(2,1)S(1)}, u32[]{:S(2)}, u32[]{:S(2)}) %all-to-all-start) | async-done | bytes 2097184 | tf_op jit(solution)/shard_map/all_to_all | solution.py:23
  42.4 1.5 copy.61
  43.9 3.5 fusion.15
  47.4 1.2 copy.62
  48.7 7.5 %fusion.2 = bf16[64,256,128]{2,1,0:T(8,128)(2,1)} fusion(bf16[64,128,2,128]{1,0,3,2:T(8,128)(2,1)S(1)} %bitcast.222, bf16[1,128,256]{1,2,0:T(8,128)(2,1)S(1)} %get-tuple-element.35, bf16[1,128,256]{1,2,0:T(8,128)(2,1)S(1)} %get-tuple-element.34), kind=kOutput, calls=%fused_computation.12 | convolution fusion | flops 1076101120 | bytes 8519680 | tf_op jit(solution)/shard_map/ijck,cjb->ibk/dot_general | solution.py:45
  56.1 6.9 %reshape.86 = bf16[64,2,16384]{2,1,0:T(2,128)(2,1)} reshape(bf16[64,256,128]{2,1,0:T(8,128)(2,1)} %fusion.2) | data formatting | bytes 8388608 | tf_op jit(solution)/shard_map/reshape | solution.py:46
  63.0 6.6 %copy.84 = bf16[64,2,16384]{2,0,1:T(8,128)(2,1)} copy(bf16[64,2,16384]{2,1,0:T(2,128)(2,1)} %reshape.86) | data formatting | bytes 8388608 | tf_op jit(solution)/shard_map/reshape | solution.py:46
  69.6 1.3 fusion.14
  70.9 1.2 copy.63
  72.2 7.4 %fusion.3 = bf16[64,256,128]{2,1,0:T(8,128)(2,1)} fusion(bf16[64,128,2,128]{1,0,3,2:T(8,128)(2,1)S(1)} %bitcast.223, bf16[1,128,256]{1,2,0:T(8,128)(2,1)S(1)} %get-tuple-element.39, bf16[1,128,256]{1,2,0:T(8,128)(2,1)S(1)} %get-tuple-element.38), kind=kOutput, calls=%fused_computation.13 | convolution fusion | flops 1076101120 | bytes 8519680 | tf_op jit(solution)/shard_map/ijck,cjb->ibk/dot_general | solution.py:45
  79.6 6.9 %reshape.88 = bf16[64,2,16384]{2,1,0:T(2,128)(2,1)} reshape(bf16[64,256,128]{2,1,0:T(8,128)(2,1)} %fusion.3) | data formatting | bytes 8388608 | tf_op jit(solution)/shard_map/reshape | solution.py:46
  86.5 6.6 %copy.83 = bf16[64,2,16384]{2,0,1:T(8,128)(2,1)} copy(bf16[64,2,16384]{2,1,0:T(2,128)(2,1)} %reshape.88) | data formatting | bytes 8388608 | tf_op jit(solution)/shard_map/reshape | solution.py:46
  93.1 6.2 %pad_maximum_fusion = bf16[2,2,64,16384]{3,2,1,0:T(8,128)(2,1)} fusion(bf16[2,1,64,16384]{3,2,1,0:T(8,128)(2,1)} %bitcast.226, bf16[2,1,64,16384]{3,2,1,0:T(8,128)(2,1)S(1)} %bitcast.224), kind=kLoop, calls=%fused_computation.9 | loop fusion | flops 4194304 | bytes 16777216 | tf_op jit(solution)/shard_map/stack | solution.py:54
  99.3 34.5 %copy.50 = bf16[2,2,64,16384]{2,1,0,3:T(2,128)(2,1)} copy(bf16[2,2,64,16384]{3,2,1,0:T(8,128)(2,1)} %pad_maximum_fusion) | data formatting | bytes 16777216 | tf_op jit(solution)/shard_map/stack | solution.py:54
  133.7 26.7 %reshape.135 = bf16[32,2,65536]{2,1,0:T(2,128)(2,1)} reshape(bf16[16384,2,2,64]{3,2,1,0:T(2,128)(2,1)} %bitcast.215) | data formatting | bytes 16777216
  160.4 5.4 %all-to-all-start.1 = ((bf16[32,2,65536]{2,1,0:T(2,128)(2,1)}), bf16[32,2,65536]{2,1,0:T(2,128)(2,1)}, u32[]{:S(2)}, u32[]{:S(2)}) async-start(bf16[32,2,65536]{2,1,0:T(2,128)(2,1)} %reshape.135), calls=%async_computation.1 | async-start | bytes 16777216 | tf_op jit(solution)/shard_map/all_to_all | solution.py:55
  165.9 5.8 %fusion.56 = (bf16[2,1,2048,512]{3,2,1,0:T(8,128)(2,1)}, bf16[2,1,2048,512]{3,2,1,0:T(8,128)(2,1)}) fusion(bf16[2,2,2048,512]{3,2,1,0:T(8,128)(2,1)} %param.8), kind=kLoop, calls=%fused_computation.112 | loop fusion | bytes 16777216 | tf_op jit(solution)/shard_map/slice | solution.py:59
  171.7 4.9 %gather_fusion.3 = bf16[16,2,128,512]{3,2,1,0:T(8,128)(2,1)} fusion(bf16[2,16,128,512]{3,2,1,0:T(8,128)(2,1)} %bitcast.227, s32[1024]{0:T(1024)S(1)} %pad_clamp_fusion), kind=kCustom, calls=%fused_computation.clone | custom fusion | bytes 8388672 | tf_op jit(solution)/shard_map/jit(_take)/gather | solution.py:60
  176.6 5.0 %gather_fusion.4 = bf16[16,2,128,512]{3,2,1,0:T(8,128)(2,1)} fusion(bf16[2,16,128,512]{3,2,1,0:T(8,128)(2,1)} %bitcast.225, s32[1024]{0:T(1024)S(1)} %pad_clamp_fusion), kind=kCustom, calls=%fused_computation.1.clone | custom fusion | bytes 8388672 | tf_op jit(solution)/shard_map/jit(_take)/gather | solution.py:60
  182.3 5.9 %fusion.5 = (bf16[2,16,128,512]{3,2,1,0:T(8,128)(2,1)}, bf16[2,16,128,512]{3,2,1,0:T(8,128)(2,1)}) fusion(bf16[16,2,128,512]{3,2,1,0:T(8,128)(2,1)} %gather_fusion.3, pred[16]{0:T(512)(128)(4,1)S(1)} %compare_and_fusion, bf16[16,2,128,512]{3,2,1,0:T(8,128)(2,1)} %gather_fusion.4), kind=kLoop, calls=%fused_computation.17 | loop fusion | flops 4194304 | bytes 16777232 | tf_op jit(solution)/shard_map/jit(_take)/select_n | solution.py:60
  189.6 1.8 copy.43
  193.7 1.6 copy_convert_fusion.1
  195.2 1.6 copy_convert_fusion
  196.8 75.8 %all-to-all-done.1 = bf16[32,2,65536]{2,1,0:T(2,128)(2,1)} async-done(((bf16[32,2,65536]{2,1,0:T(2,128)(2,1)}), bf16[32,2,65536]{2,1,0:T(2,128)(2,1)}, u32[]{:S(2)}, u32[]{:S(2)}) %all-to-all-start.1) | async-done | bytes 8388640 | tf_op jit(solution)/shard_map/all_to_all | solution.py:55
  272.6 26.0 %reshape.136 = bf16[16384,2,2,64]{3,2,1,0:T(2,128)(2,1)} reshape(bf16[32,2,65536]{2,1,0:T(2,128)(2,1)} %all-to-all-done.1) | data formatting | bytes 16777216
  298.7 36.0 %copy.51 = bf16[2,2,32,64,512]{4,3,2,1,0:T(8,128)(2,1)} copy(bf16[2,2,32,64,512]{3,1,0,4,2:T(2,128)(2,1)} %bitcast.216) | data formatting | bytes 16777216 | tf_op jit(solution)/shard_map/all_to_all | solution.py:55
  334.7 4.0 fusion.55
  341.5 1.4 copy-done.2
  348.4 75.7 %psum.7 = f32[2,1,2,16,1]{3,2,0,4,1:T(2,128)S(1)} all-reduce(f32[2,1,2,16,1]{3,2,0,4,1:T(2,128)S(1)} %bitcast.236), channel_id=1, replica_groups=mesh['tm'=4,'op'=32] {'op'}, use_global_device_ids=true, to_apply=%region_4.6 | all-reduce | flops 64 | bytes 512 | tf_op jit(solution)/shard_map/psum | solution.py:80
  (53 shorter events, 16.6 us)
Async XLA Ops:
  0.0 12.1 %copy-start.7 = (s32[16,1]{0,1:T(1,128)S(1)}, s32[16,1]{0,1:T(1,128)}, u32[]{:S(2)}) copy-start(s32[16,1]{0,1:T(1,128)} %param.10) | copy-start | bytes 196
  0.0 14.6 %copy-start = (s32[16,3]{0,1:T(4,128)S(1)}, s32[16,3]{0,1:T(4,128)}, u32[]{:S(2)}) copy-start(s32[16,3]{0,1:T(4,128)} %param.11) | copy-start | bytes 580
  2.5 37.9 %all-to-all-start = ((bf16[32,2,1,2,16,512]{5,4,3,1,2,0:T(8,128)(2,1)}), bf16[32,2,1,2,16,512]{5,4,3,1,2,0:T(8,128)(2,1)S(1)}, u32[]{:S(2)}, u32[]{:S(2)}) async-start(bf16[32,2,1,2,16,512]{5,4,3,1,2,0:T(8,128)(2,1)} %stack.48), calls=%async_computation | async-start | bytes 4194304 | tf_op jit(solution)/shard_map/all_to_all | solution.py:23
  63.0 6.6 %copy-start.1 = (bf16[2,8192,128]{2,1,0:T(8,128)(2,1)S(1)}, bf16[2,8192,128]{2,1,0:T(8,128)(2,1)}, u32[]{:S(2)}) copy-start(bf16[2,8192,128]{2,1,0:T(8,128)(2,1)} %reshape_squeeze.19) | copy-start | bytes 12582916
  86.5 6.6 %copy-start.4 = (bf16[64,2,16384]{2,0,1:T(8,128)(2,1)S(1)}, bf16[64,2,16384]{2,0,1:T(8,128)(2,1)}, u32[]{:S(2)}) copy-start(bf16[64,2,16384]{2,0,1:T(8,128)(2,1)} %copy.84) | copy-start | bytes 12582916
  160.4 112.2 %all-to-all-start.1 = ((bf16[32,2,65536]{2,1,0:T(2,128)(2,1)}), bf16[32,2,65536]{2,1,0:T(2,128)(2,1)}, u32[]{:S(2)}, u32[]{:S(2)}) async-start(bf16[32,2,65536]{2,1,0:T(2,128)(2,1)} %reshape.135), calls=%async_computation.1 | async-start | bytes 16777216 | tf_op jit(solution)/shard_map/all_to_all | solution.py:55
  334.7 4.7 %copy-start.3 = (bf16[2,16,128,512]{3,2,1,0:T(8,128)(2,1)S(1)}, bf16[2,16,128,512]{3,2,1,0:T(8,128)(2,1)}, u32[]{:S(2)}) copy-start(bf16[2,16,128,512]{3,2,1,0:T(8,128)(2,1)} %get-tuple-element.48) | copy-start | bytes 12582916
  340.8 2.2 copy-start.2
  344.4 1.6 copy-start.6
  346.0 1.6 copy-start.5
